TPU v7x, 256 devices: a whole 4x4x8 slice. The times are simulated.
256 devices in a mesh: ket: 16 (over x, y_hi, core), bra: 16 (over z, y_lo).
Axes of the slice: x: 4, y: 4 (y_hi: 2, y_lo: 2; y = y_hi * 2 + y_lo), z: 8, core: 2. Of those that a mesh axis runs over, the one named last changes fastest.
Arguments:
- density: bfloat16 [2, 2, 12288, 12288], P(None, None, 'ket', 'bra'), may hold values from -6 to 6
- coupling: bfloat16 [48, 3, 256, 256], P('bra'), may hold values from -0.21875 to 0.21875
- block_cols: int32 [48, 3], replicated, may hold values from 0 to 47, as said below
- block_count: int32 [48], replicated, may hold values from 2 to 3, as said below
- energies: float32 [12288], replicated, may hold values from -0.5 to 97
Outputs:
- dissipated: bfloat16 [2, 2, 12288, 12288], P(None, None, 'ket', 'bra')
Inputs may be any that keep to these rules, and one draw needn't show every extreme that they name: Row i of block_cols holds i - 1, i and i + 1 in some order; entries that would lie outside 0 to 47 stand last and are replaced by i. Slots k < block_count[i] name distinct blocks. block_count[i] is at most the number of block columns of i - 1, i, i + 1 inside the grid.
All inputs are finite; a program needn't handle non-finite values.
Results may differ from a plain program's by a relative error of at most 0.0054.
Values may be sent and summed in bfloat16 or wider, within the bound.
A program may use at most 320 MiB of HBM per device.

v0:
```python
import jax
import jax.numpy as jnp
from jax import lax
from jax.sharding import PartitionSpec as P

thermal_beta_factor = 1.0
frequency_cutoff_scale = 4.0


def broadcast(value, axis, source):
    kept = jnp.where(lax.axis_index(axis) == source, value, 0).astype(value.dtype)
    return lax.psum(kept, axis)


def with_halo(block, sides, width):
    for axis, dim in sides:
        count = lax.axis_size(axis)
        forward = [(i, i + 1) for i in range(count - 1)]
        backward = [(target, source) for source, target in forward]
        low = lax.ppermute(
            lax.slice_in_dim(block, block.shape[dim] - width, None, axis=dim), axis, forward
        )
        high = lax.ppermute(lax.slice_in_dim(block, 0, width, axis=dim), axis, backward)
        block = jnp.concatenate([low, block, high], axis=dim)
    return block


def weigh(matrix, start_block, block_cols, block_count, energies):
    row_count = matrix.shape[0]
    slots = matrix.shape[1]
    block_size = matrix.shape[2]
    block_total = block_cols.shape[0]
    position = start_block + jnp.arange(row_count, dtype=jnp.int32)
    inside = (position >= 0) & (position < block_total)
    clamped = jnp.clip(position, 0, block_total - 1)
    columns = jnp.take(block_cols, clamped, axis=0)
    counts = jnp.take(block_count, clamped, axis=0)
    kept_levels = (jnp.arange(slots, dtype=jnp.int32)[None, :] < counts[:, None]) & inside[:, None]
    levels = energies.reshape(block_total, block_size)
    row_levels = jnp.take(levels, clamped, axis=0)
    col_levels = jnp.take(levels, columns.reshape(-1), axis=0).reshape(row_count, slots, block_size)
    energy_detuning = row_levels[:, None, :, None] - col_levels[:, :, None, :]
    spectral_density = jax.nn.sigmoid(thermal_beta_factor * energy_detuning) * jnp.exp(
        -jnp.abs(energy_detuning) / frequency_cutoff_scale
    )
    held = kept_levels[:, :, None, None]
    operator = jnp.where(held, matrix, jnp.zeros_like(matrix))
    weighted = jnp.where(
        held, matrix.astype(jnp.float32) * spectral_density, jnp.float32(0.0)
    ).astype(jnp.bfloat16)
    return (operator, weighted, columns)


def left_apply(matrix, columns, start_block, source_operator):
    copies, halves, source_rows, breadth = source_operator.shape
    row_count, slots, block_size = (matrix.shape[0], matrix.shape[1], matrix.shape[2])
    pieces = source_operator.reshape(copies, halves, source_rows // block_size, block_size, breadth)
    relative = (columns - start_block).reshape(-1)
    picked = jnp.take(pieces, relative, axis=2).reshape(
        copies, halves, row_count, slots, block_size, breadth
    )
    result = jnp.einsum("ikab,rpikbc->rpiac", matrix, picked, preferred_element_type=jnp.float32)
    return result.reshape(copies, halves, row_count * block_size, breadth)


def right_apply(matrix, columns, start_block, source_operator):
    copies, halves, source_rows, breadth = source_operator.shape
    row_count, slots, block_size = (matrix.shape[0], matrix.shape[1], matrix.shape[2])
    pieces = source_operator.reshape(copies, halves, source_rows, breadth // block_size, block_size)
    relative = (columns - start_block).reshape(-1)
    picked = jnp.take(pieces, relative, axis=3).reshape(
        copies, halves, source_rows, row_count, slots, block_size
    )
    result = jnp.einsum("rpxjkb,jkab->rpxja", picked, matrix, preferred_element_type=jnp.float32)
    return result.reshape(copies, halves, source_rows, row_count * block_size)


def body(density, coupling, block_cols, block_count, energies):
    block_size = coupling.shape[2]
    tile_rows = density.shape[2]
    tile_cols = density.shape[3]
    row_blocks = tile_rows // block_size
    col_blocks = tile_cols // block_size
    ket_index = lax.axis_index("ket")
    bra_index = lax.axis_index("bra")
    panel_owner = ket_index * lax.axis_size("bra") // lax.axis_size("ket")
    panel = broadcast(coupling, "bra", panel_owner)
    row_start = ket_index * row_blocks
    col_start = bra_index * col_blocks
    bordered = with_halo(density, (("ket", 2), ("bra", 3)), block_size)
    row_operator, row_weighted, row_columns = weigh(
        panel, row_start, block_cols, block_count, energies
    )
    col_operator, col_weighted, col_columns = weigh(
        coupling, col_start, block_cols, block_count, energies
    )
    commutand = (
        left_apply(
            row_weighted,
            row_columns,
            row_start - 1,
            bordered[:, :, :, block_size : block_size + tile_cols],
        )
        - right_apply(
            col_weighted,
            col_columns,
            col_start - 1,
            bordered[:, :, block_size : block_size + tile_rows, :],
        )
    ).astype(jnp.bfloat16)
    outer = with_halo(commutand, (("ket", 2), ("bra", 3)), block_size)
    dissipated = (
        right_apply(
            col_operator,
            col_columns,
            col_start - 1,
            outer[:, :, block_size : block_size + tile_rows, :],
        )
        - left_apply(
            row_operator,
            row_columns,
            row_start - 1,
            outer[:, :, :, block_size : block_size + tile_cols],
        )
    ).astype(jnp.bfloat16)
    return dissipated


def solution(mesh):
    return jax.shard_map(
        body,
        mesh=mesh,
        in_specs=(P(None, None, "ket", "bra"), P("bra", None, None, None), P(), P(), P()),
        out_specs=P(None, None, "ket", "bra"),
        check_vma=False,
    )
```

profile of v0, /device:TPU:92, one launch (start us, length us, event | category | flops | bytes accessed | tf_op | source)
XLA Modules:
  0.0 556.4 jit_solution(13479946788003193734)
XLA Ops:
  22.0 84.1 %collective-permute-done = bf16[2,2,256,768]{3,2,1,0:T(8,128)(2,1)} collective-permute-done((bf16[2,2,256,768]{3,2,1,0:T(8,128)(2,1)}, bf16[2,2,256,768]{3,2,1,0:T(8,128)(2,1)}, u32[]{:S(2)}, u32[]{:S(2)}) %collective-permute-start) | collective-permute-done | bytes 1572896 | tf_op jit(solution)/shard_map/ppermute | solution.py:20
  123.8 10.0 %gather_fusion.2 = bf16[9,2,2,256,768]{4,3,2,1,0:T(8,128)(2,1)} fusion(bf16[2,2,5,256,768]{4,3,1,0,2:T(8,128)(2,1)} %copy.31, s32[1024]{0:T(1024)S(1)} %get-tuple-element.25), kind=kCustom, calls=%fused_computation.2.clone | custom fusion | bytes 28311588 | tf_op jit(solution)/shard_map/jit(_take)/gather | solution.py:59
  133.9 10.7 %broadcast_select_fusion.3 = bf16[9,2,2,256,768]{4,3,2,1,0:T(8,128)(2,1)} fusion(bf16[9,2,2,256,768]{4,3,2,1,0:T(8,128)(2,1)} %gather_fusion.2, pred[9]{0:T(512)(128)(4,1)S(1)} %compare_and_fusion.3), kind=kLoop, calls=%fused_computation.15 | loop fusion | flops 7077888 | bytes 28311560 | tf_op jit(solution)/shard_map/jit(_take)/select_n | solution.py:59
  144.6 84.9 %all-reduce.2.cloned.1.call-done = bf16[3,3,256,256]{3,2,1,0:T(8,128)(2,1)} async-done(((bf16[3,3,256,256]{3,2,1,0:T(8,128)(2,1)}), bf16[3,3,256,256]{3,2,1,0:T(8,128)(2,1)}) %all-reduce.2.cloned.1.call-update) | async-done | bytes 1179664 | tf_op jit(solution)/shard_map/psum | solution.py:12
  229.5 9.1 %convolution_bitcast_fusion.3 = f32[2,2,3,256,768]{4,3,1,0,2:T(8,128)S(1)} fusion(bf16[2,2,3,3,256,768]{5,4,1,0,3,2:T(8,128)(2,1)} %bitcast.92, bf16[3,3,256,256]{3,2,1,0:T(8,128)(2,1)} %all-reduce.2.cloned.1.call-done, f32[3,3,256]{2,1,0:T(4,128)S(1)} %sub.69, f32[3,256]{1,0:T(4,128)S(1)} %broadcast_select_fusion.8, pred[3,3]{1,0:T(4,128)(4,1)S(1)} %fusion.47), kind=kOutput, calls=%fused_computation.30 | convolution fusion | flops 3630956544 | bytes 24784904 | tf_op jit(solution)/shard_map/ikab,rpikbc->rpiac/dot_general | solution.py:62
  243.4 6.7 %pad_maximum_fusion.4 = bf16[2,2,768,1280]{3,2,1,0:T(8,128)(2,1)} fusion(bf16[2,2,1280,256]{3,2,1,0:T(8,128)(2,1)} %collective-permute-done.3, bf16[2,2,1280,768]{3,2,1,0:T(8,128)(2,1)} %copy-done.3, bf16[2,2,1280,256]{3,2,1,0:T(8,128)(2,1)} %collective-permute-done.2), kind=kLoop, calls=%fused_computation.24 | loop fusion | flops 23592960 | bytes 20971520 | tf_op jit(solution)/shard_map/concatenate | solution.py:24
  250.1 10.7 %copy.35 = bf16[2,2,768,1280]{2,3,1,0:T(8,128)(2,1)} copy(bf16[2,2,768,1280]{3,2,1,0:T(8,128)(2,1)} %pad_maximum_fusion.4) | data formatting | bytes 15728640 | tf_op jit(solution)/shard_map/slice | solution.py:108
  260.7 7.1 %copy.36 = bf16[2,2,768,5,256]{2,4,1,0,3:T(8,128)(2,1)} copy(bf16[2,2,768,5,256]{2,4,3,1,0:T(8,128)(2,1)} %bitcast.90) | data formatting | bytes 15728640 | tf_op jit(solution)/shard_map/reshape | solution.py:69
  267.8 10.0 %gather_fusion.9 = bf16[9,2,2,768,256]{3,4,2,1,0:T(8,128)(2,1)} fusion(bf16[2,2,768,5,256]{2,4,1,0,3:T(8,128)(2,1)} %copy.36, s32[1024]{0:T(1024)S(1)} %pad_clamp_fusion), kind=kCustom, calls=%fused_computation.5.clone | custom fusion | bytes 28311588 | tf_op jit(solution)/shard_map/jit(_take)/gather | solution.py:71
  277.8 7.1 %broadcast_select_fusion = bf16[9,2,2,768,256]{3,4,2,1,0:T(8,128)(2,1)S(1)} fusion(bf16[9,2,2,768,256]{3,4,2,1,0:T(8,128)(2,1)} %gather_fusion.9, pred[9]{0:T(512)(128)(4,1)S(1)} %compare_and_fusion), kind=kLoop, calls=%fused_computation.12 | loop fusion | flops 7077888 | bytes 28311560 | tf_op jit(solution)/shard_map/jit(_take)/select_n | solution.py:71
  294.1 9.7 %copy.40 = f32[2,2,768,768]{3,2,1,0:T(8,128)} copy(f32[2,2,768,768]{2,3,1,0:T(8,128)} %bitcast.88) | data formatting | bytes 18874368 | tf_op jit(solution)/shard_map/reshape | solution.py:75
  303.8 10.1 %fusion.1 = bf16[2,2,768,768]{3,2,1,0:T(8,128)(2,1)} fusion(f32[2,2,768,768]{3,2,1,0:T(8,128)} %copy.40, f32[2,2,3,256,768]{4,3,2,1,0:T(8,128)} %copy.34), kind=kLoop, calls=%fused_computation.19 | loop fusion | flops 4718592 | bytes 23592960 | tf_op jit(solution)/shard_map/convert_element_type | solution.py:110
  323.4 89.7 %collective-permute-done.4 = bf16[2,2,256,768]{3,2,1,0:T(8,128)(2,1)S(1)} collective-permute-done((bf16[2,2,256,768]{3,2,1,0:T(8,128)(2,1)S(1)}, bf16[2,2,256,768]{3,2,1,0:T(8,128)(2,1)S(1)}, u32[]{:S(2)}, u32[]{:S(2)}) %collective-permute-start.4) | collective-permute-done | bytes 1572896 | tf_op jit(solution)/shard_map/ppermute | solution.py:20
  426.4 10.0 %gather_fusion.11 = bf16[9,2,2,256,768]{4,3,2,1,0:T(8,128)(2,1)} fusion(bf16[2,2,5,256,768]{4,3,2,1,0:T(8,128)(2,1)} %bitcast.86, s32[1024]{0:T(1024)S(1)} %get-tuple-element.25), kind=kCustom, calls=%fused_computation.8.clone | custom fusion | bytes 28311588 | tf_op jit(solution)/shard_map/jit(_take)/gather | solution.py:59
  436.4 7.0 %broadcast_select_fusion.2 = bf16[9,2,2,256,768]{4,3,2,1,0:T(8,128)(2,1)S(1)} fusion(bf16[9,2,2,256,768]{4,3,2,1,0:T(8,128)(2,1)} %gather_fusion.11, pred[9]{0:T(512)(128)(4,1)S(1)} %compare_and_fusion.3), kind=kLoop, calls=%fused_computation.14 | loop fusion | flops 7077888 | bytes 28311560 | tf_op jit(solution)/shard_map/jit(_take)/select_n | solution.py:59
  453.4 9.6 %copy.49 = f32[2,2,768,768]{2,3,1,0:T(8,128)} copy(f32[2,2,768,768]{3,2,1,0:T(8,128)} %bitcast.89) | data formatting | bytes 18874368 | tf_op jit(solution)/shard_map/reshape | solution.py:63
  463.0 19.5 %collective-permute-done.6 = bf16[2,2,1280,256]{3,2,1,0:T(8,128)(2,1)} collective-permute-done((bf16[2,2,1280,256]{3,2,1,0:T(8,128)(2,1)}, bf16[2,2,1280,256]{3,2,1,0:T(8,128)(2,1)}, u32[]{:S(2)}, u32[]{:S(2)}) %collective-permute-start.6) | collective-permute-done | bytes 2621472 | tf_op jit(solution)/shard_map/ppermute | solution.py:20
  482.5 6.7 %pad_maximum_fusion = bf16[2,2,768,1280]{3,2,1,0:T(8,128)(2,1)} fusion(bf16[2,2,1280,256]{3,2,1,0:T(8,128)(2,1)} %collective-permute-done.7, bf16[2,2,1280,256]{3,2,1,0:T(8,128)(2,1)} %collective-permute-done.6, bf16[2,2,256,768]{3,2,1,0:T(8,128)(2,1)} %copy-done.5, bf16[2,2,768,768]{3,2,1,0:T(8,128)(2,1)} %fusion.1, ...), kind=kLoop, calls=%fused_computation.20 | loop fusion | flops 39321600 | bytes 20971520 | tf_op jit(solution)/shard_map/concatenate | solution.py:24
  489.2 10.7 %copy.41 = bf16[2,2,768,1280]{2,3,1,0:T(8,128)(2,1)} copy(bf16[2,2,768,1280]{3,2,1,0:T(8,128)(2,1)} %pad_maximum_fusion) | data formatting | bytes 15728640 | tf_op jit(solution)/shard_map/slice | solution.py:117
  499.9 7.1 %copy.42 = bf16[2,2,768,5,256]{2,4,1,0,3:T(8,128)(2,1)} copy(bf16[2,2,768,5,256]{2,4,3,1,0:T(8,128)(2,1)} %bitcast.91) | data formatting | bytes 15728640 | tf_op jit(solution)/shard_map/reshape | solution.py:69
  507.0 10.0 %gather_fusion.10 = bf16[9,2,2,768,256]{3,4,2,1,0:T(8,128)(2,1)} fusion(bf16[2,2,768,5,256]{2,4,1,0,3:T(8,128)(2,1)} %copy.42, s32[1024]{0:T(1024)S(1)} %pad_clamp_fusion), kind=kCustom, calls=%fused_computation.11.clone | custom fusion | bytes 28311588 | tf_op jit(solution)/shard_map/jit(_take)/gather | solution.py:71
  517.0 7.1 %broadcast_select_fusion.1 = bf16[9,2,2,768,256]{3,4,2,1,0:T(8,128)(2,1)S(1)} fusion(bf16[9,2,2,768,256]{3,4,2,1,0:T(8,128)(2,1)} %gather_fusion.10, pred[9]{0:T(512)(128)(4,1)S(1)} %compare_and_fusion), kind=kLoop, calls=%fused_computation.13 | loop fusion | flops 7077888 | bytes 28311560 | tf_op jit(solution)/shard_map/jit(_take)/select_n | solution.py:71
  532.8 10.2 %fusion = bf16[2,2,768,768]{2,3,1,0:T(8,128)(2,1)} fusion(f32[2,2,768,768]{2,3,1,0:T(8,128)} %copy.49, f32[2,2,768,3,256]{2,4,3,1,0:T(8,128)} %copy.45), kind=kLoop, calls=%fused_computation.17 | loop fusion | flops 4718592 | bytes 23592960 | tf_op jit(solution)/shard_map/convert_element_type | solution.py:125
  542.9 6.6 %copy.50 = bf16[2,2,768,768]{3,2,1,0:T(8,128)(2,1)} copy(bf16[2,2,768,768]{2,3,1,0:T(8,128)(2,1)} %fusion) | data formatting | bytes 9437184 | tf_op jit(solution)/shard_map/convert_element_type | solution.py:125
  (96 shorter events, 88.3 us)
Async XLA Ops:
  6.5 12.7 %copy-start = (s32[48]{0:T(128)S(1)}, s32[48]{0:T(128)}, u32[]{:S(2)}) copy-start(s32[48]{0:T(128)} %param.20) | copy-start | bytes 580
  6.5 9.6 %copy-start.9 = (s32[48,3]{0,1:T(4,128)S(1)}, s32[48,3]{0,1:T(4,128)}, u32[]{:S(2)}) copy-start(s32[48,3]{0,1:T(4,128)} %param.19) | copy-start | bytes 1732
  6.5 11.3 %copy-start.8 = (f32[12288]{0:T(1024)S(1)}, f32[12288]{0:T(1024)}, u32[]{:S(2)}) copy-start(f32[12288]{0:T(1024)} %param.21) | copy-start | bytes 147460
  6.5 223.0 %all-reduce.2.cloned.1.call-start = ((), (), s32[]{:S(2)}) async-start(), calls=%async_computation | async-start | bytes 2359296 | tf_op jit(solution)/shard_map/psum | solution.py:12
  11.5 98.8 %collective-permute-start.1 = (bf16[2,2,256,768]{3,2,1,0:T(8,128)(2,1)}, bf16[2,2,256,768]{3,2,1,0:T(8,128)(2,1)S(1)}, u32[]{:S(2)}, u32[]{:S(2)}) collective-permute-start(bf16[2,2,256,768]{3,2,1,0:T(8,128)(2,1)} %get-tuple-element.21), channel_id=1, source_target_pairs={{16,0},{32,16},{48,32},{64,48},{80,64},{96,80},{112,96},{128,112},... | collective-permute-start | bytes 4718600 | tf_op jit(solution)/shard_map/ppermute | solution.py:23
  14.1 92.0 %collective-permute-start = (bf16[2,2,256,768]{3,2,1,0:T(8,128)(2,1)}, bf16[2,2,256,768]{3,2,1,0:T(8,128)(2,1)}, u32[]{:S(2)}, u32[]{:S(2)}) collective-permute-start(bf16[2,2,256,768]{3,2,1,0:T(8,128)(2,1)} %get-tuple-element.22), channel_id=1, source_target_pairs={{0,16},{16,32},{32,48},{48,64},{64,80},{80,96},{96,112},{112,128},... | collective-permute-start | bytes 4718600 | tf_op jit(solution)/shard_map/ppermute | solution.py:20
  110.5 13.4 %copy-start.3 = (bf16[2,2,1280,768]{3,2,1,0:T(8,128)(2,1)}, bf16[2,2,1280,768]{3,2,1,0:T(8,128)(2,1)S(1)}, u32[]{:S(2)}) copy-start(bf16[2,2,1280,768]{3,2,1,0:T(8,128)(2,1)S(1)} %constant_dynamic-update-slice_fusion) | copy-start | bytes 23592964
  113.4 130.0 %collective-permute-start.2 = (bf16[2,2,1280,256]{3,2,1,0:T(8,128)(2,1)}, bf16[2,2,1280,256]{3,2,1,0:T(8,128)(2,1)}, u32[]{:S(2)}, u32[]{:S(2)}) collective-permute-start(bf16[2,2,1280,256]{3,2,1,0:T(8,128)(2,1)} %get-tuple-element.17), channel_id=1, source_target_pairs={{0,1},{1,2},{2,3},{3,4},{4,5},{5,6},{6,7},{7,8},{8,9},{9,10},{10,1... | collective-permute-start | bytes 7864328 | tf_op jit(solution)/shard_map/ppermute | solution.py:20
  116.8 126.6 %collective-permute-start.3 = (bf16[2,2,1280,256]{3,2,1,0:T(8,128)(2,1)}, bf16[2,2,1280,256]{3,2,1,0:T(8,128)(2,1)}, u32[]{:S(2)}, u32[]{:S(2)}) collective-permute-start(bf16[2,2,1280,256]{3,2,1,0:T(8,128)(2,1)} %get-tuple-element.18), channel_id=1, source_target_pairs={{1,0},{2,1},{3,2},{4,3},{5,4},{6,5},{7,6},{8,7},{9,8},{10,9},{11,1... | collective-permute-start | bytes 7864328 | tf_op jit(solution)/shard_map/ppermute | solution.py:23
  277.8 7.1 %copy-start.6 = (bf16[3,3,256,256]{3,2,1,0:T(8,128)(2,1)S(1)}, bf16[3,3,256,256]{3,2,1,0:T(8,128)(2,1)}, u32[]{:S(2)}) copy-start(bf16[3,3,256,256]{3,2,1,0:T(8,128)(2,1)} %param.18) | copy-start | bytes 3538948
  313.9 100.3 %copy-start.4 = (bf16[2,2,768,768]{3,2,1,0:T(8,128)(2,1)S(1)}, bf16[2,2,768,768]{3,2,1,0:T(8,128)(2,1)}, u32[]{:S(2)}) copy-start(bf16[2,2,768,768]{3,2,1,0:T(8,128)(2,1)} %fusion.1) | copy-start | bytes 14155780
  316.2 96.9 %collective-permute-start.4 = (bf16[2,2,256,768]{3,2,1,0:T(8,128)(2,1)S(1)}, bf16[2,2,256,768]{3,2,1,0:T(8,128)(2,1)S(1)}, u32[]{:S(2)}, u32[]{:S(2)}) collective-permute-start(bf16[2,2,256,768]{3,2,1,0:T(8,128)(2,1)S(1)} %get-tuple-element.19), channel_id=1, source_target_pairs={{0,16},{16,32},{32,48},{48,64},{64,80},{80,96},{96,112},{112,128},... | collective-permute-start | bytes 4718600 | tf_op jit(solution)/shard_map/ppermute | solution.py:20
  318.2 94.9 %collective-permute-start.5 = (bf16[2,2,256,768]{3,2,1,0:T(8,128)(2,1)S(1)}, bf16[2,2,256,768]{3,2,1,0:T(8,128)(2,1)S(1)}, u32[]{:S(2)}, u32[]{:S(2)}) collective-permute-start(bf16[2,2,256,768]{3,2,1,0:T(8,128)(2,1)S(1)} %get-tuple-element.20), channel_id=1, source_target_pairs={{16,0},{32,16},{48,32},{64,48},{80,64},{96,80},{112,96},{128,112},... | collective-permute-start | bytes 4718600 | tf_op jit(solution)/shard_map/ppermute | solution.py:23
  413.1 1.1 copy-start.5
  414.8 3.1 copy-start.2
  420.6 61.9 %collective-permute-start.6 = (bf16[2,2,1280,256]{3,2,1,0:T(8,128)(2,1)}, bf16[2,2,1280,256]{3,2,1,0:T(8,128)(2,1)}, u32[]{:S(2)}, u32[]{:S(2)}) collective-permute-start(bf16[2,2,1280,256]{3,2,1,0:T(8,128)(2,1)} %get-tuple-element.14), channel_id=1, source_target_pairs={{0,1},{1,2},{2,3},{3,4},{4,5},{5,6},{6,7},{7,8},{8,9},{9,10},{10,1... | collective-permute-start | bytes 7864328 | tf_op jit(solution)/shard_map/ppermute | solution.py:20
  422.5 60.0 %collective-permute-start.7 = (bf16[2,2,1280,256]{3,2,1,0:T(8,128)(2,1)}, bf16[2,2,1280,256]{3,2,1,0:T(8,128)(2,1)}, u32[]{:S(2)}, u32[]{:S(2)}) collective-permute-start(bf16[2,2,1280,256]{3,2,1,0:T(8,128)(2,1)} %get-tuple-element.16), channel_id=1, source_target_pairs={{1,0},{2,1},{3,2},{4,3},{5,4},{6,5},{7,6},{8,7},{9,8},{10,9},{11,1... | collective-permute-start | bytes 7864328 | tf_op jit(solution)/shard_map/ppermute | solution.py:23
  517.0 7.1 %copy-start.7 = (bf16[3,3,256,256]{3,2,1,0:T(8,128)(2,1)S(1)}, bf16[3,3,256,256]{3,2,1,0:T(8,128)(2,1)}, u32[]{:S(2)}) copy-start(bf16[3,3,256,256]{3,2,1,0:T(8,128)(2,1)} %param.18) | copy-start | bytes 3538948
  532.8 16.8 %copy-start.1 = (s32[48]{0:T(128)S(1)}, s32[48]{0:T(128)}, u32[]{:S(2)}) copy-start(s32[48]{0:T(128)} %param.20) | copy-start | bytes 580
Sparse Core Ops, SparseCore 0:
  10.0 219.4 all-reduce.1
where the time goes:
time: 558 us; the launch traced here: 556 us
  waiting for transfers between devices  278 us (50%)
  local copies, waits for them, and re-layouts  149 us (27%)
  other arithmetic  67.9 us (12%)
  starting transfers between devices  24.3 us (4%)
  matrix products  22.6 us (4%)
  between operations  13.8 us (2%)
    ppermute x4, waiting for transfers between devices, with_halo(): lax.ppermute(lax.slice_in_dim(block, block.shape[dim] - width, None, axis...  193 us
    psum x1, waiting for transfers between devices, broadcast(): return lax.psum(kept, axis)  84.9 us
    gather x2, local copies, waits for them, and re-layouts, left_apply(): jnp.take(pieces, relative, axis=2)  20 us
    gather x2, local copies, waits for them, and re-layouts, right_apply(): jnp.take(pieces, relative, axis=3)  20 us
    select_n x3, other arithmetic, left_apply(): jnp.take(pieces, relative, axis=2)  17.7 us
    ppermute x4, starting transfers between devices, with_halo(): lax.ppermute(lax.slice_in_dim(block, 0, width, axis=dim), axis, backward)  15 us
    dot_general x2, matrix products, left_apply(): jnp.einsum('ikab,rpikbc->rpiac', matrix, picked, preferred_element_type=j...  14.3 us
    reshape x2, local copies, waits for them, and re-layouts, right_apply(): source_operator.reshape(copies, halves, source_rows, breadth // block_siz...  14.1 us
  transfers between devices with their start and end apart: 9, of which 4 were waited for; matrix products, arithmetic and copies ran while one was open for 16% of the time, Pallas kernels for 0%

commit v1 on v0

--- a/solution.py
+++ b/solution.py
@@ -9,7 +9,7 @@
 
 def broadcast(value, axis, source):
     kept = jnp.where(lax.axis_index(axis) == source, value, 0).astype(value.dtype)
-    return lax.psum(kept, axis)
+    return jnp.sum(jax.lax.all_gather(kept, axis_name=axis), 0)
 
 
 def with_halo(block, sides, width):

time: 558 us -> 830 us (1.49)
  the two profiles are of different devices: /device:TPU:92 before, /device:TPU:45 now
where the time goes in v1:
time: 830 us; the launch traced here: 828 us
  waiting for transfers between devices  542 us (65%)
  local copies, waits for them, and re-layouts  150 us (18%)
  other arithmetic  77 us (9%)
  matrix products  23 us (3%)
  starting transfers between devices  22.6 us (3%)
  between operations  13.8 us (2%)
    ppermute x4, waiting for transfers between devices, with_halo(): lax.ppermute(lax.slice_in_dim(block, block.shape[dim] - width, None, axis...  352 us
    all_gather x1, waiting for transfers between devices, broadcast(): return jnp.sum(jax.lax.all_gather(kept, axis_name=axis), 0)  126 us
    ppermute x4, waiting for transfers between devices, with_halo(): lax.ppermute(lax.slice_in_dim(block, 0, width, axis=dim), axis, backward)  65.1 us
    gather x2, local copies, waits for them, and re-layouts, right_apply(): jnp.take(pieces, relative, axis=3)  20.3 us
    gather x2, local copies, waits for them, and re-layouts, left_apply(): jnp.take(pieces, relative, axis=2)  20 us
    select_n x3, other arithmetic, left_apply(): jnp.take(pieces, relative, axis=2)  17.9 us
  transfers between devices with their start and end apart: 9, of which 6 were waited for; matrix products, arithmetic and copies ran while one was open for 17% of the time, Pallas kernels for 0%

profile of v1, /device:TPU:45, one launch (start us, length us, event | category | flops | bytes accessed | tf_op | source)
XLA Modules:
  0.0 828.3 jit_solution(10584637982654994003)
XLA Ops:
  24.3 145.8 %collective-permute-done = bf16[2,2,256,768]{3,2,1,0:T(8,128)(2,1)} collective-permute-done((bf16[2,2,256,768]{3,2,1,0:T(8,128)(2,1)}, bf16[2,2,256,768]{3,2,1,0:T(8,128)(2,1)}, u32[]{:S(2)}, u32[]{:S(2)}) %collective-permute-start) | collective-permute-done | bytes 1572896 | tf_op jit(solution)/shard_map/ppermute | solution.py:20
  186.6 10.0 %gather_fusion.2 = bf16[9,2,2,256,768]{4,3,2,1,0:T(8,128)(2,1)} fusion(bf16[2,2,5,256,768]{4,3,1,0,2:T(8,128)(2,1)} %copy.53, s32[1024]{0:T(1024)S(1)} %get-tuple-element.25), kind=kCustom, calls=%fused_computation.2.clone | custom fusion | bytes 28311588 | tf_op jit(solution)/shard_map/jit(_take)/gather | solution.py:59
  196.6 10.9 %broadcast_select_fusion.3 = bf16[9,2,2,256,768]{4,3,2,1,0:T(8,128)(2,1)} fusion(bf16[9,2,2,256,768]{4,3,2,1,0:T(8,128)(2,1)} %gather_fusion.2, pred[9]{0:T(512)(128)(4,1)S(1)} %compare_and_fusion.3), kind=kLoop, calls=%fused_computation.15 | loop fusion | flops 7077888 | bytes 28311560 | tf_op jit(solution)/shard_map/jit(_take)/select_n | solution.py:59
  207.5 154.7 %collective-permute-done.2 = bf16[2,2,1280,256]{3,2,1,0:T(8,128)(2,1)} collective-permute-done((bf16[2,2,1280,256]{3,2,1,0:T(8,128)(2,1)}, bf16[2,2,1280,256]{3,2,1,0:T(8,128)(2,1)}, u32[]{:S(2)}, u32[]{:S(2)}) %collective-permute-start.2) | collective-permute-done | bytes 2621472 | tf_op jit(solution)/shard_map/ppermute | solution.py:20
  367.8 10.6 %copy.57 = bf16[2,2,768,1280]{2,3,1,0:T(8,128)(2,1)} copy(bf16[2,2,768,1280]{3,2,1,0:T(8,128)(2,1)} %pad_maximum_fusion.4) | data formatting | bytes 15728640 | tf_op jit(solution)/shard_map/slice | solution.py:108
  378.4 7.1 copy.58
  385.5 10.1 %gather_fusion.9 = bf16[9,2,2,768,256]{3,4,2,1,0:T(8,128)(2,1)} fusion(bf16[2,2,768,5,256]{2,4,1,0,3:T(8,128)(2,1)} %copy.58, s32[1024]{0:T(1024)S(1)} %pad_clamp_fusion), kind=kCustom, calls=%fused_computation.5.clone | custom fusion | bytes 28311588 | tf_op jit(solution)/shard_map/jit(_take)/gather | solution.py:71
  395.6 7.1 broadcast_select_fusion
  412.0 9.6 %copy.62 = f32[2,2,768,768]{3,2,1,0:T(8,128)} copy(f32[2,2,768,768]{2,3,1,0:T(8,128)} %bitcast.89) | data formatting | bytes 18874368 | tf_op jit(solution)/shard_map/reshape | solution.py:75
  421.6 125.6 %all-gather.3.cloned.1.call-done = bf16[48,3,256,256]{3,2,1,0:T(8,128)(2,1)} async-done(((bf16[3,3,256,256]{3,2,1,0:T(8,128)(2,1)}), bf16[48,3,256,256]{3,2,1,0:T(8,128)(2,1)}) %all-gather.3.cloned.1.call-update) | async-done | bytes 18874384 | tf_op jit(solution)/shard_map/all_gather | solution.py:12
  547.2 10.2 %reduce_sum.12 = bf16[3,3,256,256]{3,2,1,0:T(8,128)(2,1)S(1)} reduce(bf16[16,3,3,256,256]{4,3,2,1,0:T(8,128)(2,1)} %bitcast.93, bf16[]{:T(256)} %constant.78.clone.1), dimensions={0}, to_apply=%region_0.0 | reduce | flops 8847360 | bytes 20054018 | tf_op jit(solution)/shard_map/reduce_sum | solution.py:12
  557.4 9.5 %convolution_bitcast_fusion.3 = f32[2,2,3,256,768]{4,3,1,0,2:T(8,128)S(1)} fusion(bf16[2,2,3,3,256,768]{5,4,1,0,3,2:T(8,128)(2,1)} %bitcast.94, bf16[3,3,256,256]{3,2,1,0:T(8,128)(2,1)S(1)} %reduce_sum.12, f32[3,3,256]{2,1,0:T(4,128)S(1)} %sub.69, f32[3,256]{1,0:T(4,128)S(1)} %broadcast_select_fusion.8, pred[3,3]{1,0:T(4,128)(4,1)S(1)} %fusion.47), kind=kOutput, calls=%fused_computation.30 | convolution fusion | flops 3630956544 | bytes 24784904 | tf_op jit(solution)/shard_map/ikab,rpikbc->rpiac/dot_general | solution.py:62
  571.7 10.1 %fusion.1 = bf16[2,2,768,768]{3,2,1,0:T(8,128)(2,1)} fusion(f32[2,2,768,768]{3,2,1,0:T(8,128)} %copy.62, f32[2,2,3,256,768]{4,3,2,1,0:T(8,128)} %copy.56), kind=kLoop, calls=%fused_computation.19 | loop fusion | flops 4718592 | bytes 23592960 | tf_op jit(solution)/shard_map/convert_element_type | solution.py:110
  588.8 32.2 %collective-permute-done.4 = bf16[2,2,256,768]{3,2,1,0:T(8,128)(2,1)S(1)} collective-permute-done((bf16[2,2,256,768]{3,2,1,0:T(8,128)(2,1)S(1)}, bf16[2,2,256,768]{3,2,1,0:T(8,128)(2,1)S(1)}, u32[]{:S(2)}, u32[]{:S(2)}) %collective-permute-start.4) | collective-permute-done | bytes 1572896 | tf_op jit(solution)/shard_map/ppermute | solution.py:20
  621.0 65.1 %collective-permute-done.5 = bf16[2,2,256,768]{3,2,1,0:T(8,128)(2,1)S(1)} collective-permute-done((bf16[2,2,256,768]{3,2,1,0:T(8,128)(2,1)S(1)}, bf16[2,2,256,768]{3,2,1,0:T(8,128)(2,1)S(1)}, u32[]{:S(2)}, u32[]{:S(2)}) %collective-permute-start.5) | collective-permute-done | bytes 1572896 | tf_op jit(solution)/shard_map/ppermute | solution.py:23
  698.8 10.0 %gather_fusion.11 = bf16[9,2,2,256,768]{4,3,2,1,0:T(8,128)(2,1)} fusion(bf16[2,2,5,256,768]{4,3,2,1,0:T(8,128)(2,1)} %bitcast.87, s32[1024]{0:T(1024)S(1)} %get-tuple-element.25), kind=kCustom, calls=%fused_computation.8.clone | custom fusion | bytes 28311588 | tf_op jit(solution)/shard_map/jit(_take)/gather | solution.py:59
  708.8 7.0 broadcast_select_fusion.2
  725.8 9.7 %copy.71 = f32[2,2,768,768]{2,3,1,0:T(8,128)} copy(f32[2,2,768,768]{3,2,1,0:T(8,128)} %bitcast.90) | data formatting | bytes 18874368 | tf_op jit(solution)/shard_map/reshape | solution.py:63
  735.4 18.9 %collective-permute-done.6 = bf16[2,2,1280,256]{3,2,1,0:T(8,128)(2,1)} collective-permute-done((bf16[2,2,1280,256]{3,2,1,0:T(8,128)(2,1)}, bf16[2,2,1280,256]{3,2,1,0:T(8,128)(2,1)}, u32[]{:S(2)}, u32[]{:S(2)}) %collective-permute-start.6) | collective-permute-done | bytes 2621472 | tf_op jit(solution)/shard_map/ppermute | solution.py:20
  761.2 10.6 %copy.63 = bf16[2,2,768,1280]{2,3,1,0:T(8,128)(2,1)} copy(bf16[2,2,768,1280]{3,2,1,0:T(8,128)(2,1)} %pad_maximum_fusion) | data formatting | bytes 15728640 | tf_op jit(solution)/shard_map/slice | solution.py:117
  771.8 7.1 copy.64
  778.9 10.2 %gather_fusion.10 = bf16[9,2,2,768,256]{3,4,2,1,0:T(8,128)(2,1)} fusion(bf16[2,2,768,5,256]{2,4,1,0,3:T(8,128)(2,1)} %copy.64, s32[1024]{0:T(1024)} %copy-done.11), kind=kCustom, calls=%fused_computation.11.clone | custom fusion | bytes 28311588 | tf_op jit(solution)/shard_map/jit(_take)/gather | solution.py:71
  789.1 7.1 broadcast_select_fusion.1
  804.8 10.1 %fusion = bf16[2,2,768,768]{2,3,1,0:T(8,128)(2,1)} fusion(f32[2,2,768,768]{2,3,1,0:T(8,128)} %copy.71, f32[2,2,768,3,256]{2,4,3,1,0:T(8,128)} %copy.67), kind=kLoop, calls=%fused_computation.17 | loop fusion | flops 4718592 | bytes 23592960 | tf_op jit(solution)/shard_map/convert_element_type | solution.py:125
  (107 shorter events, 105.5 us)
Async XLA Ops:
  6.5 12.0 %copy-start = (s32[48]{0:T(128)S(1)}, s32[48]{0:T(128)}, u32[]{:S(2)}) copy-start(s32[48]{0:T(128)} %param.20) | copy-start | bytes 580
  6.5 13.4 %copy-start.12 = (s32[48,3]{0,1:T(4,128)S(1)}, s32[48,3]{0,1:T(4,128)}, u32[]{:S(2)}) copy-start(s32[48,3]{0,1:T(4,128)} %param.19) | copy-start | bytes 1732
  6.5 14.6 %copy-start.10 = (f32[12288]{0:T(1024)S(1)}, f32[12288]{0:T(1024)}, u32[]{:S(2)}) copy-start(f32[12288]{0:T(1024)} %param.21) | copy-start | bytes 147460
  6.5 540.7 %all-gather.3.cloned.1.call-start = ((), (), s32[]{:S(2)}) async-start(), calls=%async_computation | async-start | bytes 20054016 | tf_op jit(solution)/shard_map/all_gather | solution.py:12
  11.5 162.8 %collective-permute-start.1 = (bf16[2,2,256,768]{3,2,1,0:T(8,128)(2,1)}, bf16[2,2,256,768]{3,2,1,0:T(8,128)(2,1)S(1)}, u32[]{:S(2)}, u32[]{:S(2)}) collective-permute-start(bf16[2,2,256,768]{3,2,1,0:T(8,128)(2,1)} %get-tuple-element.21), channel_id=1, source_target_pairs={{16,0},{32,16},{48,32},{64,48},{80,64},{96,80},{112,96},{128,112},... | collective-permute-start | bytes 4718600 | tf_op jit(solution)/shard_map/ppermute | solution.py:23
  14.1 156.0 %collective-permute-start = (bf16[2,2,256,768]{3,2,1,0:T(8,128)(2,1)}, bf16[2,2,256,768]{3,2,1,0:T(8,128)(2,1)}, u32[]{:S(2)}, u32[]{:S(2)}) collective-permute-start(bf16[2,2,256,768]{3,2,1,0:T(8,128)(2,1)} %get-tuple-element.22), channel_id=1, source_target_pairs={{0,16},{16,32},{32,48},{48,64},{64,80},{80,96},{96,112},{112,128},... | collective-permute-start | bytes 4718600 | tf_op jit(solution)/shard_map/ppermute | solution.py:20
  24.2 361.3 %copy-start.11 = (s32[1024]{0:T(1024)}, s32[1024]{0:T(1024)S(1)}, u32[]{:S(2)}) copy-start(s32[1024]{0:T(1024)S(1)} %pad_clamp_fusion) | copy-start | bytes 12292
  24.2 371.4 %copy-start.13 = (pred[9]{0:T(512)(128)(4,1)}, pred[9]{0:T(512)(128)(4,1)S(1)}, u32[]{:S(2)}) copy-start(pred[9]{0:T(512)(128)(4,1)S(1)} %compare_and_fusion) | copy-start | bytes 31
  174.4 12.3 %copy-start.3 = (bf16[2,2,1280,768]{3,2,1,0:T(8,128)(2,1)}, bf16[2,2,1280,768]{3,2,1,0:T(8,128)(2,1)S(1)}, u32[]{:S(2)}) copy-start(bf16[2,2,1280,768]{3,2,1,0:T(8,128)(2,1)S(1)} %constant_dynamic-update-slice_fusion) | copy-start | bytes 23592964
  177.3 185.0 %collective-permute-start.2 = (bf16[2,2,1280,256]{3,2,1,0:T(8,128)(2,1)}, bf16[2,2,1280,256]{3,2,1,0:T(8,128)(2,1)}, u32[]{:S(2)}, u32[]{:S(2)}) collective-permute-start(bf16[2,2,1280,256]{3,2,1,0:T(8,128)(2,1)} %get-tuple-element.17), channel_id=1, source_target_pairs={{0,1},{1,2},{2,3},{3,4},{4,5},{5,6},{6,7},{7,8},{8,9},{9,10},{10,1... | collective-permute-start | bytes 7864328 | tf_op jit(solution)/shard_map/ppermute | solution.py:20
  179.2 183.0 %collective-permute-start.3 = (bf16[2,2,1280,256]{3,2,1,0:T(8,128)(2,1)}, bf16[2,2,1280,256]{3,2,1,0:T(8,128)(2,1)}, u32[]{:S(2)}, u32[]{:S(2)}) collective-permute-start(bf16[2,2,1280,256]{3,2,1,0:T(8,128)(2,1)} %get-tuple-element.18), channel_id=1, source_target_pairs={{1,0},{2,1},{3,2},{4,3},{5,4},{6,5},{7,6},{8,7},{9,8},{10,9},{11,1... | collective-permute-start | bytes 7864328 | tf_op jit(solution)/shard_map/ppermute | solution.py:23
  196.6 165.6 %copy-start.4 = (bf16[2,2,1280,768]{3,2,1,0:T(8,128)(2,1)S(1)}, bf16[2,2,1280,768]{3,2,1,0:T(8,128)(2,1)}, u32[]{:S(2)}) copy-start(bf16[2,2,1280,768]{3,2,1,0:T(8,128)(2,1)} %copy-done.3) | copy-start | bytes 23592964
  395.6 7.1 copy-start.8
  557.4 9.5 %copy-start.7 = (bf16[3,3,256,256]{3,2,1,0:T(8,128)(2,1)}, bf16[3,3,256,256]{3,2,1,0:T(8,128)(2,1)S(1)}, u32[]{:S(2)}) copy-start(bf16[3,3,256,256]{3,2,1,0:T(8,128)(2,1)S(1)} %reduce_sum.12) | copy-start | bytes 3538948
  581.7 105.5 %copy-start.5 = (bf16[2,2,768,768]{3,2,1,0:T(8,128)(2,1)S(1)}, bf16[2,2,768,768]{3,2,1,0:T(8,128)(2,1)}, u32[]{:S(2)}) copy-start(bf16[2,2,768,768]{3,2,1,0:T(8,128)(2,1)} %fusion.1) | copy-start | bytes 14155780
  584.0 37.0 %collective-permute-start.4 = (bf16[2,2,256,768]{3,2,1,0:T(8,128)(2,1)S(1)}, bf16[2,2,256,768]{3,2,1,0:T(8,128)(2,1)S(1)}, u32[]{:S(2)}, u32[]{:S(2)}) collective-permute-start(bf16[2,2,256,768]{3,2,1,0:T(8,128)(2,1)S(1)} %get-tuple-element.19), channel_id=1, source_target_pairs={{0,16},{16,32},{32,48},{48,64},{64,80},{80,96},{96,112},{112,128},... | collective-permute-start | bytes 4718600 | tf_op jit(solution)/shard_map/ppermute | solution.py:20
  586.8 99.3 %collective-permute-start.5 = (bf16[2,2,256,768]{3,2,1,0:T(8,128)(2,1)S(1)}, bf16[2,2,256,768]{3,2,1,0:T(8,128)(2,1)S(1)}, u32[]{:S(2)}, u32[]{:S(2)}) collective-permute-start(bf16[2,2,256,768]{3,2,1,0:T(8,128)(2,1)S(1)} %get-tuple-element.20), channel_id=1, source_target_pairs={{16,0},{32,16},{48,32},{64,48},{80,64},{96,80},{112,96},{128,112},... | collective-permute-start | bytes 4718600 | tf_op jit(solution)/shard_map/ppermute | solution.py:23
  686.1 1.2 copy-start.6
  687.8 3.1 copy-start.2
  693.6 60.8 %collective-permute-start.6 = (bf16[2,2,1280,256]{3,2,1,0:T(8,128)(2,1)}, bf16[2,2,1280,256]{3,2,1,0:T(8,128)(2,1)}, u32[]{:S(2)}, u32[]{:S(2)}) collective-permute-start(bf16[2,2,1280,256]{3,2,1,0:T(8,128)(2,1)} %get-tuple-element.14), channel_id=1, source_target_pairs={{0,1},{1,2},{2,3},{3,4},{4,5},{5,6},{6,7},{7,8},{8,9},{9,10},{10,1... | collective-permute-start | bytes 7864328 | tf_op jit(solution)/shard_map/ppermute | solution.py:20
  695.5 58.9 %collective-permute-start.7 = (bf16[2,2,1280,256]{3,2,1,0:T(8,128)(2,1)}, bf16[2,2,1280,256]{3,2,1,0:T(8,128)(2,1)}, u32[]{:S(2)}, u32[]{:S(2)}) collective-permute-start(bf16[2,2,1280,256]{3,2,1,0:T(8,128)(2,1)} %get-tuple-element.16), channel_id=1, source_target_pairs={{1,0},{2,1},{3,2},{4,3},{5,4},{6,5},{7,6},{8,7},{9,8},{10,9},{11,1... | collective-permute-start | bytes 7864328 | tf_op jit(solution)/shard_map/ppermute | solution.py:23
  778.9 10.2 %copy-start.14 = (pred[9]{0:T(512)(128)(4,1)S(1)}, pred[9]{0:T(512)(128)(4,1)}, u32[]{:S(2)}) copy-start(pred[9]{0:T(512)(128)(4,1)} %copy-done.13) | copy-start | bytes 31
  789.1 7.1 copy-start.9
  804.8 16.7 %copy-start.1 = (s32[48]{0:T(128)S(1)}, s32[48]{0:T(128)}, u32[]{:S(2)}) copy-start(s32[48]{0:T(128)} %param.20) | copy-start | bytes 580
Sparse Core Ops, SparseCore 0:
  9.2 538.0 all-gather.2
